TPU v7x, 32 devices: a whole 2x2x4 slice. The times are simulated.
32 devices in a mesh: shard: 4 (over x, core), context: 4 (over z), tensor: 2 (over y).
Axes of the slice: x: 2, y: 2, z: 4, core: 2. Of those that a mesh axis runs over, the one named last changes fastest.
Arguments:
- layer_input: bfloat16 [4, 2048, 1024], P('shard', 'context'), may hold values from -5 to 5
- segment_ids: int32 [4, 2048], P('shard'), may hold values from 0 to 3, never falling along the last dimension, each value on 1 to 1024 neighbouring positions
- out_grad: bfloat16 [4, 2048, 1024], P('shard', ('context', 'tensor')), may hold values from -6 to 6
- attn_in: float32 [3, 1024, 1024], P(None, 'shard', 'tensor'), may hold values from -0.1875 to 0.1875
- attn_out: float32 [1024, 1024], P('tensor', 'shard'), may hold values from -0.75 to 0.75
- mlp_up: float32 [1024, 4096], P('shard', 'tensor'), may hold values from -0.1875 to 0.1875
- mlp_down: float32 [4096, 1024], P('tensor', 'shard'), may hold values from -0.09375 to 0.09375
- vectors: float32 [8, 1024], replicated, may hold values from -0.8 to 1.4, as said below
- up_bias: float32 [4096], replicated, may hold values from -0.8 to 0.8
- attn_in_moments: float32 [2, 3, 1024, 1024], P(None, None, 'shard', 'tensor'), may hold values from -1.44 to 1.44, as said below
- attn_out_moments: float32 [2, 1024, 1024], P(None, 'tensor', 'shard'), may hold values from -3.6 to 3.6, as said below
- mlp_up_moments: float32 [2, 1024, 4096], P(None, 'shard', 'tensor'), may hold values from -2.16 to 2.16, as said below
- mlp_down_moments: float32 [2, 4096, 1024], P(None, 'tensor', 'shard'), may hold values from -4.32 to 4.32, as said below
- vector_moments: float32 [2, 8, 1024], replicated, may hold values from -7.2 to 7.2, as said below
- up_bias_moments: float32 [2, 4096], replicated, may hold values from -2.16 to 2.16, as said below
Outputs:
- block_output: bfloat16 [4, 2048, 1024], P('shard', ('context', 'tensor'))
- input_grad: bfloat16 [4, 2048, 1024], P('shard', ('context', 'tensor'))
- attn_in_grad: float32 [3, 1024, 1024], P(None, 'shard', 'tensor')
- attn_out_grad: float32 [1024, 1024], P('tensor', 'shard')
- mlp_up_grad: float32 [1024, 4096], P('shard', 'tensor')
- mlp_down_grad: float32 [4096, 1024], P('tensor', 'shard')
- vectors_grad: float32 [8, 1024], replicated
- up_bias_grad: float32 [4096], replicated
- attn_in_new: float32 [3, 1024, 1024], P(None, 'shard', 'tensor')
- attn_out_new: float32 [1024, 1024], P('tensor', 'shard')
- mlp_up_new: float32 [1024, 4096], P('shard', 'tensor')
- mlp_down_new: float32 [4096, 1024], P('tensor', 'shard')
- vectors_new: float32 [8, 1024], replicated
- up_bias_new: float32 [4096], replicated
- attn_in_moments_new: float32 [2, 3, 1024, 1024], P(None, None, 'shard', 'tensor')
- attn_out_moments_new: float32 [2, 1024, 1024], P(None, 'tensor', 'shard')
- mlp_up_moments_new: float32 [2, 1024, 4096], P(None, 'shard', 'tensor')
- mlp_down_moments_new: float32 [2, 4096, 1024], P(None, 'tensor', 'shard')
- vector_moments_new: float32 [2, 8, 1024], replicated
- up_bias_moments_new: float32 [2, 4096], replicated
Inputs may be any that keep to these rules, and one draw needn't show every extreme that they name: `vectors`: rows 4 and 6 are gains near one, the others biases near zero. `attn_in_moments`: index 0 holds first moments, index 1 positive second moments. `attn_out_moments`: index 0 holds first moments, index 1 positive second moments. `mlp_up_moments`: index 0 holds first moments, index 1 positive second moments. `mlp_down_moments`: index 0 holds first moments, index 1 positive second moments. `vector_moments`: index 0 holds first moments, index 1 positive second moments. `up_bias_moments`: index 0 holds first moments, index 1 positive second moments.
All inputs are finite; a program needn't handle non-finite values.
Results may differ from a plain program's by a relative error of at most 0.023.
Values may be sent and summed in bfloat16 or wider, within the bound.
No kernel may reach another device: no remote copies, remote signals or barrier semaphores. Data moves between devices by JAX's collectives and lax.ppermute only.
A program may use at most 256 MiB of HBM per device.

v0:
```python
import jax
import jax.numpy as jnp
from jax import lax
from jax.sharding import PartitionSpec as P

HD = 64
layer_eps = 1e-05
beta_one = 0.9
beta_two = 0.999
adam_eps = 1e-06
learning_rate = 0.02
weight_decay = 0.01
adam_step = 3.0
masked_score = -1e30


def normalize(hidden):
    center = hidden - jnp.mean(hidden, axis=-1, keepdims=True)
    scale = lax.rsqrt(jnp.mean(center * center, axis=-1, keepdims=True) + layer_eps)
    return (center * scale, scale)


def norm_back(upstream, normed, scale, gain):
    scaled = upstream * gain
    return scale * (
        scaled
        - jnp.mean(scaled, axis=-1, keepdims=True)
        - normed * jnp.mean(scaled * normed, axis=-1, keepdims=True)
    )


def gelu_value(value):
    return 0.5 * value * (1.0 + jax.scipy.special.erf(value * 0.7071067811865476))


def gelu_slope(value):
    return (
        0.5 * (1.0 + jax.scipy.special.erf(value * 0.7071067811865476))
        + value * jnp.exp(-0.5 * value * value) * 0.3989422804014327
    )


def adamw(param, moments, grad, decay):
    first = beta_one * moments[0] + (1.0 - beta_one) * grad
    second = beta_two * moments[1] + (1.0 - beta_two) * grad * grad
    update = (
        first
        / (1.0 - beta_one**adam_step)
        / (jnp.sqrt(second / (1.0 - beta_two**adam_step)) + adam_eps)
    )
    return (param - learning_rate * (update + decay * param), jnp.stack([first, second]))


def inner_rows(left, right):
    return lax.dot_general(
        left, right, (((0,), (0,)), ((), ())), preferred_element_type=jnp.float32
    )


def against_rows(left, right):
    return lax.dot_general(
        left, right, (((1,), (1,)), ((), ())), preferred_element_type=jnp.float32
    )


def over_context(grads):
    return (
        lax.psum(grads[0].astype(jnp.bfloat16), "context").astype(jnp.float32),
        lax.psum(grads[1].astype(jnp.bfloat16), "context").astype(jnp.float32),
        lax.psum(grads[2].astype(jnp.bfloat16), "context").astype(jnp.float32),
        lax.psum(grads[3].astype(jnp.bfloat16), "context").astype(jnp.float32),
    )


def to_owner(grads):
    return (
        lax.psum_scatter(
            grads[0].astype(jnp.bfloat16), "shard", scatter_dimension=1, tiled=True
        ).astype(jnp.float32),
        lax.psum_scatter(
            grads[1].astype(jnp.bfloat16), "shard", scatter_dimension=1, tiled=True
        ).astype(jnp.float32),
        lax.psum_scatter(
            grads[2].astype(jnp.bfloat16), "shard", scatter_dimension=0, tiled=True
        ).astype(jnp.float32),
        lax.psum_scatter(
            grads[3].astype(jnp.bfloat16), "shard", scatter_dimension=1, tiled=True
        ).astype(jnp.float32),
    )


def on_device(
    layer_input,
    segment_ids,
    out_grad,
    attn_in,
    attn_out,
    mlp_up,
    mlp_down,
    vectors,
    up_bias,
    attn_in_moments,
    attn_out_moments,
    mlp_up_moments,
    mlp_down_moments,
    vector_moments,
    up_bias_moments,
):
    tensor_count = lax.axis_size("tensor")
    tensor_rank = lax.axis_index("tensor")
    context_rank = lax.axis_index("context")
    seq_count = layer_input.shape[0]
    count_rows = layer_input.shape[1]
    model_width = vectors.shape[1]
    tokens = jnp.transpose(layer_input, (1, 0, 2)).reshape(count_rows * seq_count, model_width)
    all_rows = count_rows * seq_count
    share_tok = count_rows // tensor_count
    share_rows = share_tok * seq_count
    head_width = attn_in.shape[2]
    hidden_width = mlp_up.shape[1]
    length = segment_ids.shape[1]
    head_count = head_width // HD
    scale = 1.0 / HD**0.5
    in_full, out_full, up_full, down_full = (
        lax.all_gather(attn_in.astype(jnp.bfloat16), "shard", axis=1, tiled=True),
        lax.all_gather(attn_out.astype(jnp.bfloat16), "shard", axis=1, tiled=True),
        lax.all_gather(mlp_up.astype(jnp.bfloat16), "shard", axis=0, tiled=True),
        lax.all_gather(mlp_down.astype(jnp.bfloat16), "shard", axis=1, tiled=True),
    )
    head_start = tensor_rank * head_width
    unit_start = tensor_rank * hidden_width
    query_bias = lax.dynamic_slice_in_dim(vectors[0], head_start, head_width)
    value_bias = lax.dynamic_slice_in_dim(vectors[1], head_start, head_width)
    unit_bias = lax.dynamic_slice_in_dim(up_bias, unit_start, hidden_width)
    project = jnp.einsum("td,kdh->kth", tokens, in_full, preferred_element_type=jnp.float32)
    query_half = (project[0] + query_bias).astype(jnp.bfloat16)
    key_half = project[1].astype(jnp.bfloat16).reshape(count_rows, seq_count, head_width)
    value_half = (
        (project[2] + value_bias).astype(jnp.bfloat16).reshape(count_rows, seq_count, head_width)
    )
    keys_all, values_all = (
        lax.all_gather(key_half, "context", axis=0, tiled=True),
        lax.all_gather(value_half, "context", axis=0, tiled=True),
    )
    query_seq = query_half.reshape(count_rows, seq_count, head_count, HD)
    block = min(512, count_rows)
    blocks = count_rows // block

    def scores_of(which, lower):
        key_heads = keys_all[:, which].reshape(length, head_count, HD)
        segment = segment_ids[which]
        own_segment = lax.dynamic_slice_in_dim(segment, context_rank * count_rows, count_rows)
        raw = (
            jnp.einsum(
                "qhd,khd->hqk",
                query_seq[lower : lower + block, which],
                key_heads,
                preferred_element_type=jnp.float32,
            )
            * scale
        )
        same = own_segment[:, None] == segment[None, :]
        return jnp.where(same[None], raw, masked_score)

    which = 0
    value_heads = values_all[:, which].reshape(length, head_count, HD)
    parts = []
    index = 0
    raw = scores_of(which, index * block)
    top = jnp.max(raw, axis=-1, keepdims=True)
    total = top + jnp.log(jnp.sum(jnp.exp(raw - top), axis=-1, keepdims=True))
    attend = jnp.exp(raw - total).astype(jnp.bfloat16)
    parts.append(
        jnp.einsum("hqk,khd->qhd", attend, value_heads, preferred_element_type=jnp.float32).reshape(
            block, head_width
        )
    )
    totals = [total]
    seq_contexts = [parts[0]]
    context = jnp.stack(seq_contexts, 1).reshape(all_rows, head_width)
    context_half = context.astype(jnp.bfloat16)
    my_start = tensor_rank * share_rows
    attn_share = lax.psum_scatter(
        jnp.dot(context_half, out_full, preferred_element_type=jnp.float32).astype(jnp.bfloat16),
        "tensor",
        scatter_dimension=0,
        tiled=True,
    ).astype(jnp.float32)
    residual_in = lax.dynamic_slice_in_dim(tokens, my_start, share_rows, 0).astype(jnp.float32)
    normed_one, scale_one = normalize(residual_in + attn_share + vectors[2])
    first = normed_one * vectors[4] + vectors[5]
    first_all = lax.all_gather(first.astype(jnp.bfloat16), "tensor", axis=0, tiled=True)
    before = jnp.dot(first_all, up_full, preferred_element_type=jnp.float32) + unit_bias
    hidden_half = gelu_value(before).astype(jnp.bfloat16)
    mlp_share = lax.psum_scatter(
        jnp.dot(hidden_half, down_full, preferred_element_type=jnp.float32).astype(jnp.bfloat16),
        "tensor",
        scatter_dimension=0,
        tiled=True,
    ).astype(jnp.float32)
    normed_two, scale_two = normalize(first + mlp_share + vectors[3])
    block_output = (normed_two * vectors[6] + vectors[7]).astype(jnp.bfloat16)
    upstream = (
        jnp.transpose(out_grad, (1, 0, 2)).reshape(share_rows, model_width).astype(jnp.float32)
    )
    grad_two = norm_back(upstream, normed_two, scale_two, vectors[6])
    grad_two_all = lax.all_gather(grad_two.astype(jnp.bfloat16), "tensor", axis=0, tiled=True)
    down_grad = inner_rows(hidden_half, grad_two_all)
    grad_before = against_rows(grad_two_all, down_full) * gelu_slope(before)
    grad_before_half = grad_before.astype(jnp.bfloat16)
    up_grad = inner_rows(first_all, grad_before_half)
    grad_first = grad_two + lax.psum_scatter(
        against_rows(grad_before_half, up_full).astype(jnp.bfloat16),
        "tensor",
        scatter_dimension=0,
        tiled=True,
    ).astype(jnp.float32)
    grad_one = norm_back(grad_first, normed_one, scale_one, vectors[4])
    grad_one_all = lax.all_gather(grad_one.astype(jnp.bfloat16), "tensor", axis=0, tiled=True)
    out_grad_w = inner_rows(context_half, grad_one_all)
    grad_context = against_rows(grad_one_all, out_full).astype(jnp.bfloat16)
    grad_seq = grad_context.reshape(count_rows, seq_count, head_count, HD)
    delta = jnp.sum(
        grad_seq.astype(jnp.float32) * context.reshape(count_rows, seq_count, head_count, HD),
        axis=-1,
    )
    which = 0
    key_heads = keys_all[:, which].reshape(length, head_count, HD)
    value_heads = values_all[:, which].reshape(length, head_count, HD)
    parts = []
    index = 0
    lower = index * block
    raw = scores_of(which, lower)
    attend_full = jnp.exp(raw - totals[which * blocks + index])
    attend = attend_full.astype(jnp.bfloat16)
    part = grad_seq[lower : lower + block, which]
    shift = jnp.transpose(delta[lower : lower + block, which])[:, :, None]
    grad_probs = jnp.einsum("qhd,khd->hqk", part, value_heads, preferred_element_type=jnp.float32)
    grad_score = (attend_full * (grad_probs - shift) * scale).astype(jnp.bfloat16)
    parts.append(
        jnp.einsum(
            "hqk,khd->qhd", grad_score, key_heads, preferred_element_type=jnp.float32
        ).reshape(block, head_width)
    )
    key_acc = jnp.einsum(
        "hqk,qhd->khd",
        grad_score,
        query_seq[lower : lower + block, which],
        preferred_element_type=jnp.float32,
    )
    value_acc = jnp.einsum("hqk,qhd->khd", attend, part, preferred_element_type=jnp.float32)
    query_list = [parts[0]]
    key_list = [key_acc.reshape(length, head_width)]
    value_list = [value_acc.reshape(length, head_width)]
    query_grad = jnp.stack(query_list, 1).reshape(all_rows, head_width)
    key_own, value_own = (
        lax.psum_scatter(
            jnp.stack(key_list, 1).astype(jnp.bfloat16), "context", scatter_dimension=0, tiled=True
        ).astype(jnp.float32),
        lax.psum_scatter(
            jnp.stack(value_list, 1).astype(jnp.bfloat16),
            "context",
            scatter_dimension=0,
            tiled=True,
        ).astype(jnp.float32),
    )
    key_own = key_own.reshape(all_rows, head_width)
    value_own = value_own.reshape(all_rows, head_width)
    stacked = jnp.stack([query_grad, key_own, value_own]).astype(jnp.bfloat16)
    in_grad = jnp.einsum("td,kth->kdh", tokens, stacked, preferred_element_type=jnp.float32)
    input_share = grad_one + lax.psum_scatter(
        jnp.einsum("kth,kdh->td", stacked, in_full, preferred_element_type=jnp.float32).astype(
            jnp.bfloat16
        ),
        "tensor",
        scatter_dimension=0,
        tiled=True,
    ).astype(jnp.float32)
    input_grad = jnp.transpose(
        input_share.astype(jnp.bfloat16).reshape(share_tok, seq_count, model_width), (1, 0, 2)
    )
    output_block = jnp.transpose(block_output.reshape(share_tok, seq_count, model_width), (1, 0, 2))
    query_row = lax.dynamic_update_slice(
        jnp.zeros((model_width,), jnp.float32), jnp.sum(query_grad, 0), (head_start,)
    )
    value_row = lax.dynamic_update_slice(
        jnp.zeros((model_width,), jnp.float32), jnp.sum(value_own, 0), (head_start,)
    )
    local_vectors = jnp.stack(
        [
            query_row,
            value_row,
            jnp.sum(grad_one, 0),
            jnp.sum(grad_two, 0),
            jnp.sum(grad_first * normed_one, 0),
            jnp.sum(grad_first, 0),
            jnp.sum(upstream * normed_two, 0),
            jnp.sum(upstream, 0),
        ]
    )
    local_bias = lax.dynamic_update_slice(
        jnp.zeros((up_bias.shape[0],), jnp.float32), jnp.sum(grad_before, 0), (unit_start,)
    )
    vector_grad, bias_grad = lax.psum((local_vectors, local_bias), ("shard", "context", "tensor"))
    local_grads = (in_grad, out_grad_w, up_grad, down_grad)
    owned = to_owner(over_context(local_grads))
    in_sum, out_sum, up_sum, down_sum = owned
    in_new, in_moments = adamw(attn_in, attn_in_moments, in_sum, weight_decay)
    out_new, out_moments = adamw(attn_out, attn_out_moments, out_sum, weight_decay)
    up_new, up_moments = adamw(mlp_up, mlp_up_moments, up_sum, weight_decay)
    down_new, down_moments = adamw(mlp_down, mlp_down_moments, down_sum, weight_decay)
    vec_new, vec_moments = adamw(vectors, vector_moments, vector_grad, 0.0)
    bias_new, bias_moments = adamw(up_bias, up_bias_moments, bias_grad, 0.0)
    return (
        output_block,
        input_grad,
        in_sum,
        out_sum,
        up_sum,
        down_sum,
        vector_grad,
        bias_grad,
        in_new,
        out_new,
        up_new,
        down_new,
        vec_new,
        bias_new,
        in_moments,
        out_moments,
        up_moments,
        down_moments,
        vec_moments,
        bias_moments,
    )


def solution(mesh):
    in_specs = (
        P("shard", "context", None),
        P("shard", None),
        P("shard", ("context", "tensor"), None),
        P(None, "shard", "tensor"),
        P("tensor", "shard"),
        P("shard", "tensor"),
        P("tensor", "shard"),
        P(),
        P(),
        P(None, None, "shard", "tensor"),
        P(None, "tensor", "shard"),
        P(None, "shard", "tensor"),
        P(None, "tensor", "shard"),
        P(),
        P(),
    )
    out_specs = (
        P("shard", ("context", "tensor"), None),
        P("shard", ("context", "tensor"), None),
        P(None, "shard", "tensor"),
        P("tensor", "shard"),
        P("shard", "tensor"),
        P("tensor", "shard"),
        P(),
        P(),
        P(None, "shard", "tensor"),
        P("tensor", "shard"),
        P("shard", "tensor"),
        P("tensor", "shard"),
        P(),
        P(),
        P(None, None, "shard", "tensor"),
        P(None, "tensor", "shard"),
        P(None, "shard", "tensor"),
        P(None, "tensor", "shard"),
        P(),
        P(),
    )
    return jax.shard_map(
        on_device, mesh=mesh, in_specs=in_specs, out_specs=out_specs, check_vma=False
    )
```

profile of v0, /device:TPU:0, one launch (start us, length us, event | category | flops | bytes accessed | tf_op | source)
XLA Modules:
  0.0 855.1 jit_solution(14302809599329487599)
XLA Ops:
  10.2 31.7 %all-gather.11.cloned.1.call-done = bf16[3,1024,512]{1,2,0:T(8,128)(2,1)} async-done(((bf16[3,256,512]{1,2,0:T(8,128)(2,1)}), bf16[3,1024,512]{1,2,0:T(8,128)(2,1)}) %all-gather.11.cloned.1.call-update) | async-done | bytes 3145744 | tf_op jit(solution)/shard_map/all_gather | solution.py:125
  54.6 39.4 %all-gather.27.cloned.1.call-done = bf16[1,2048,512]{1,2,0:T(8,128)(2,1)} async-done(((bf16[1,512,512]{1,2,0:T(8,128)(2,1)}), bf16[1,2048,512]{1,2,0:T(8,128)(2,1)}) %all-gather.27.cloned.1.call-update) | async-done | bytes 2097168 | tf_op jit(solution)/shard_map/all_gather | solution.py:142
  94.0 16.0 %fusion.1 = (f32[8,512]{1,0:T(8,128)S(1)}, f32[8,512,2048]{2,1,0:T(8,128)}) fusion(pred[512,2048]{1,0:T(8,128)(4,1)S(1)} %broadcast_compare_fusion, bf16[2048,8,64]{0,2,1:T(8,128)(2,1)} %bitcast.208, f32[512,8,64]{0,2,1:T(8,128)} %bitcast.9, f32[8,64]{1,0:T(8,128)S(1)} %add.261), kind=kOutput, calls=%fused_computation.5 | convolution fusion | flops 1099427840 | bytes 37767168 | tf_op jit(solution)/shard_map/qhd,khd->hqk/dot_general | solution.py:154
  110.0 15.1 %exponential_reduce_fusion = f32[8,512]{1,0:T(8,128)S(1)} fusion(f32[8,512,2048]{2,1,0:T(8,128)} %get-tuple-element.97, f32[8,512]{1,0:T(8,128)S(1)} %get-tuple-element.96, pred[512,2048]{1,0:T(8,128)(4,1)S(1)} %broadcast_compare_fusion), kind=kLoop, calls=%fused_computation.2 | loop fusion | flops 33550336 | bytes 34635776 | tf_op jit(solution)/shard_map/reduce_sum | solution.py:171
  125.2 15.5 %all-gather.13.cloned.1.call-done = bf16[2048,1,512]{0,2,1:T(8,128)(2,1)} async-done(((bf16[512,1,512]{0,2,1:T(8,128)(2,1)}), bf16[2048,1,512]{0,2,1:T(8,128)(2,1)}) %all-gather.13.cloned.1.call-update) | async-done | bytes 2097168 | tf_op jit(solution)/shard_map/all_gather | solution.py:143
  140.7 16.4 %fusion.57 = (bf16[512,8,64]{0,2,1:T(8,128)(2,1)S(1)}, f32[512,8,64]{0,2,1:T(8,128)}) fusion(bf16[2048,8,64]{0,2,1:T(8,128)(2,1)} %bitcast.248, f32[8,512,2048]{2,1,0:T(8,128)} %get-tuple-element.97, f32[8,512]{1,0:T(8,128)S(1)} %log_add_fusion, pred[512,2048]{1,0:T(8,128)(4,1)S(1)} %broadcast_compare_fusion), kind=kOutput, calls=%fused_computation.137 | convolution fusion | flops 1107558400 | bytes 38289408 | tf_op jit(solution)/shard_map/hqk,khd->qhd/dot_general | solution.py:174
  164.2 17.6 %reduce-scatter.11.cloned.1.call-done = bf16[256,1024]{1,0:T(8,128)(2,1)} async-done(((bf16[512,1024]{1,0:T(8,128)(2,1)}), bf16[256,1024]{1,0:T(8,128)(2,1)}) %reduce-scatter.11.cloned.1.call-update) | async-done | bytes 524304 | tf_op jit(solution)/shard_map/reduce_scatter | solution.py:183
  188.9 29.4 %all-gather.19.cloned.1.call-done = bf16[1024,2048]{1,0:T(8,128)(2,1)} async-done(((bf16[256,2048]{1,0:T(8,128)(2,1)}), bf16[1024,2048]{1,0:T(8,128)(2,1)}) %all-gather.19.cloned.1.call-update) | async-done | bytes 4194320 | tf_op jit(solution)/shard_map/all_gather | solution.py:127
  218.3 23.4 %all-gather.17.cloned.1.call-done = bf16[512,1024]{1,0:T(8,128)(2,1)} async-done(((bf16[256,1024]{1,0:T(8,128)(2,1)}), bf16[512,1024]{1,0:T(8,128)(2,1)}) %all-gather.17.cloned.1.call-update) | async-done | bytes 1048592 | tf_op jit(solution)/shard_map/all_gather | solution.py:192
  249.6 29.3 %all-gather.21.cloned.1.call-done = bf16[2048,1024]{1,0:T(8,128)(2,1)} async-done(((bf16[2048,256]{1,0:T(8,128)(2,1)}), bf16[2048,1024]{1,0:T(8,128)(2,1)}) %all-gather.21.cloned.1.call-update) | async-done | bytes 4194320 | tf_op jit(solution)/shard_map/all_gather | solution.py:128
  285.1 20.5 %reduce-scatter.13.cloned.1.call-done = bf16[256,1024]{1,0:T(8,128)(2,1)} async-done(((bf16[512,1024]{1,0:T(8,128)(2,1)}), bf16[256,1024]{1,0:T(8,128)(2,1)}) %reduce-scatter.13.cloned.1.call-update) | async-done | bytes 524304 | tf_op jit(solution)/shard_map/reduce_scatter | solution.py:195
  310.0 21.4 %all-gather.23.cloned.1.call-done = bf16[512,1024]{1,0:T(8,128)(2,1)} async-done(((bf16[256,1024]{1,0:T(8,128)(2,1)}), bf16[512,1024]{1,0:T(8,128)(2,1)}) %all-gather.23.cloned.1.call-update) | async-done | bytes 1048592 | tf_op jit(solution)/shard_map/all_gather | solution.py:207
  343.2 20.5 %reduce-scatter.15.cloned.1.call-done = bf16[256,1024]{1,0:T(8,128)(2,1)} async-done(((bf16[512,1024]{1,0:T(8,128)(2,1)}), bf16[256,1024]{1,0:T(8,128)(2,1)}) %reduce-scatter.15.cloned.1.call-update) | async-done | bytes 524304 | tf_op jit(solution)/shard_map/reduce_scatter | solution.py:212
  369.8 21.2 %all-gather.25.cloned.1.call-done = bf16[512,1024]{1,0:T(8,128)(2,1)} async-done(((bf16[256,1024]{1,0:T(8,128)(2,1)}), bf16[512,1024]{1,0:T(8,128)(2,1)}) %all-gather.25.cloned.1.call-update) | async-done | bytes 1048592 | tf_op jit(solution)/shard_map/all_gather | solution.py:219
  394.3 15.3 %convolution_convert_fusion.2 = bf16[8,64,2048]{2,1,0:T(8,128)(2,1)S(1)} fusion(bf16[512,8,64]{0,2,1:T(8,128)(2,1)} %bitcast.213, f32[8,512,2048]{2,1,0:T(8,128)} %get-tuple-element.97, f32[8,512]{1,0:T(8,128)S(1)} %log_add_fusion, pred[512,2048]{1,0:T(8,128)(4,1)S(1)} %broadcast_compare_fusion), kind=kOutput, calls=%fused_computation.22 | convolution fusion | flops 1108344832 | bytes 37240832 | tf_op jit(solution)/shard_map/hqk,qhd->khd/dot_general | solution.py:251
  412.2 17.9 %multiply_convert_fusion = bf16[8,512,2048]{2,1,0:T(8,128)(2,1)S(1)} fusion(f32[8,512,2048]{2,1,0:T(8,128)} %get-tuple-element.97, bf16[512,8,64]{0,2,1:T(8,128)(2,1)} %bitcast.214, bf16[2048,8,64]{0,2,1:T(8,128)(2,1)} %bitcast.249, f32[8,512]{1,0:T(8,128)} %bitcast.235, f32[8,512]{1,0:T(8,128)} %copy-done.46, pred[512,2048]{1,0:T(8,128)(4,1)S(1)} %broadcast_compare_fusion), kind=kOutput, calls=%fused_computation | convolution fusion | flops 1132462080 | bytes 54034432 | tf_op jit(solution)/shard_map/qhd,khd->hqk/dot_general | solution.py:238
  458.2 11.8 %fusion.55 = (f32[8,64]{1,0:T(8,128)S(1)}, bf16[512,8,64]{0,2,1:T(8,128)(2,1)}) fusion(bf16[2048,8,64]{0,2,1:T(8,128)(2,1)S(1)} %bitcast.209, bf16[8,512,2048]{2,1,0:T(8,128)(2,1)} %copy-done), kind=kOutput, calls=%fused_computation.135 | convolution fusion | flops 1074265600 | bytes 19400704 | tf_op jit(solution)/shard_map/hqk,khd->qhd/dot_general | solution.py:241
  471.3 30.2 %reduce-scatter.17.cloned.1.call-done = bf16[512,1,512]{2,0,1:T(8,128)(2,1)} async-done(((bf16[2048,1,512]{2,0,1:T(8,128)(2,1)}), bf16[512,1,512]{2,0,1:T(8,128)(2,1)}) %reduce-scatter.17.cloned.1.call-update) | async-done | bytes 524304 | tf_op jit(solution)/shard_map/reduce_scatter | solution.py:257
  512.6 15.9 %reduce-scatter.25.cloned.1.call-done = bf16[512,256]{1,0:T(8,128)(2,1)} async-done(((bf16[512,1024]{1,0:T(8,128)(2,1)}), bf16[512,256]{1,0:T(8,128)(2,1)}) %reduce-scatter.25.cloned.1.call-update) | async-done | bytes 262160 | tf_op jit(solution)/shard_map/reduce_scatter | solution.py:80
  528.5 47.4 %reduce-scatter.29.cloned.1.call-done = bf16[2048,256]{1,0:T(8,128)(2,1)} async-done(((bf16[2048,1024]{1,0:T(8,128)(2,1)}), bf16[2048,256]{1,0:T(8,128)(2,1)}) %reduce-scatter.29.cloned.1.call-update) | async-done | bytes 1048592 | tf_op jit(solution)/shard_map/reduce_scatter | solution.py:86
  575.9 47.6 %reduce-scatter.27.cloned.1.call-done = bf16[256,2048]{1,0:T(8,128)(2,1)} async-done(((bf16[1024,2048]{1,0:T(8,128)(2,1)}), bf16[256,2048]{1,0:T(8,128)(2,1)}) %reduce-scatter.27.cloned.1.call-update) | async-done | bytes 1048592 | tf_op jit(solution)/shard_map/reduce_scatter | solution.py:83
  623.4 40.7 %reduce-scatter.23.cloned.1.call-done = bf16[3,256,512]{1,2,0:T(8,128)(2,1)} async-done(((bf16[3,1024,512]{1,2,0:T(8,128)(2,1)}), bf16[3,256,512]{1,2,0:T(8,128)(2,1)}) %reduce-scatter.23.cloned.1.call-update) | async-done | bytes 786448 | tf_op jit(solution)/shard_map/reduce_scatter | solution.py:77
  673.3 41.5 %all-reduce = (f32[8,1024]{1,0:T(8,128)S(1)}, f32[4096]{0:T(1024)S(1)}) all-reduce(f32[8,1024]{1,0:T(8,128)S(1)} %stack.97, f32[4096]{0:T(1024)S(1)} %dynamic_update_slice.13), channel_id=1, replica_groups=mesh['shard'=4,'context'=4,'tensor'=2] {'shard','context','tensor'}, use_global_device_ids=true, to_apply=%region_33.34 | all-reduce | flops 12288 | bytes 98304 | tf_op jit(solution)/shard_map/psum | solution.py:304
  719.4 92.5 %all-reduce.4.cloned.1.call-done = (bf16[3,256,512]{1,2,0:T(8,128)(2,1)}, bf16[512,256]{1,0:T(8,128)(2,1)}, bf16[256,2048]{1,0:T(8,128)(2,1)}, bf16[2048,256]{1,0:T(8,128)(2,1)}) async-done(((bf16[3,256,512]{1,2,0:T(8,128)(2,1)}, bf16[512,256]{1,0:T(8,128)(2,1)}, bf16[256,2048]{1,0:T(8,128)(2,1)}, bf16[2048,256]{1,0:T(8,128)(2,1)}), (bf16[3,256,512]{1,2,0:T(8,128)(2,1)}, bf16[512,256]{1,0:T(8,128)(2,1)}, ...) | async-done | bytes 3145744 | tf_op jit(solution)/shard_map/psum | solution.py:68
  (243 shorter events, 161.6 us)
Async XLA Ops:
  7.2 34.7 %all-gather.11.cloned.1.call-start = ((), (), s32[]{:S(2)}) async-start(), calls=%async_computation.10 | async-start | bytes 3932160 | tf_op jit(solution)/shard_map/all_gather | solution.py:125
  10.1 83.9 %all-gather.27.cloned.1.call-start = ((), (), s32[]{:S(2)}) async-start(), calls=%async_computation.24 | async-start | bytes 2621440 | tf_op jit(solution)/shard_map/all_gather | solution.py:142
  48.2 92.5 %all-gather.13.cloned.1.call-start = ((), (), s32[]{:S(2)}) async-start(), calls=%async_computation.11 | async-start | bytes 2621440 | tf_op jit(solution)/shard_map/all_gather | solution.py:143
  50.5 107.8 %all-gather.15.cloned.1.call-start = ((), (), s32[]{:S(2)}) async-start(), calls=%async_computation.12 | async-start | bytes 1310720 | tf_op jit(solution)/shard_map/all_gather | solution.py:126
  51.3 130.5 %reduce-scatter.11.cloned.1.call-start = ((), (), s32[]{:S(2)}) async-start(), calls=%async_computation.13 | async-start | bytes 1572864 | tf_op jit(solution)/shard_map/reduce_scatter | solution.py:183
  125.2 269.2 %copy-start.46 = (f32[8,512]{1,0:T(8,128)}, f32[8,512]{1,0:T(8,128)S(1)}, u32[]{:S(2)}) copy-start(f32[8,512]{1,0:T(8,128)S(1)} %log_add_fusion) | copy-start | bytes 49156
  161.3 57.0 %all-gather.19.cloned.1.call-start = ((), (), s32[]{:S(2)}) async-start(), calls=%async_computation.15 | async-start | bytes 5242880 | tf_op jit(solution)/shard_map/all_gather | solution.py:127
  164.1 77.6 %all-gather.17.cloned.1.call-start = ((), (), s32[]{:S(2)}) async-start(), calls=%async_computation.14 | async-start | bytes 1572864 | tf_op jit(solution)/shard_map/all_gather | solution.py:192
  185.7 93.2 %all-gather.21.cloned.1.call-start = ((), (), s32[]{:S(2)}) async-start(), calls=%async_computation.16 | async-start | bytes 5242880 | tf_op jit(solution)/shard_map/all_gather | solution.py:128
  188.4 117.1 %reduce-scatter.13.cloned.1.call-start = ((), (), s32[]{:S(2)}) async-start(), calls=%async_computation.17 | async-start | bytes 1572864 | tf_op jit(solution)/shard_map/reduce_scatter | solution.py:195
  285.0 46.3 %all-gather.23.cloned.1.call-start = ((), (), s32[]{:S(2)}) async-start(), calls=%async_computation.18 | async-start | bytes 1572864 | tf_op jit(solution)/shard_map/all_gather | solution.py:207
  310.0 53.8 %reduce-scatter.15.cloned.1.call-start = ((), (), s32[]{:S(2)}) async-start(), calls=%async_computation.19 | async-start | bytes 1572864 | tf_op jit(solution)/shard_map/reduce_scatter | solution.py:212
  343.1 47.8 %all-gather.25.cloned.1.call-start = ((), (), s32[]{:S(2)}) async-start(), calls=%async_computation.20 | async-start | bytes 1572864 | tf_op jit(solution)/shard_map/all_gather | solution.py:219
  369.5 101.7 %reduce-scatter.19.cloned.1.call-start = ((), (), s32[]{:S(2)}) async-start(), calls=%async_computation.22 | async-start | bytes 2621440 | tf_op jit(solution)/shard_map/reduce_scatter | solution.py:260
  412.2 89.4 %reduce-scatter.17.cloned.1.call-start = ((), (), s32[]{:S(2)}) async-start(), calls=%async_computation.21 | async-start | bytes 2621440 | tf_op jit(solution)/shard_map/reduce_scatter | solution.py:257
  441.0 87.5 %reduce-scatter.25.cloned.1.call-start = ((), (), s32[]{:S(2)}) async-start(), calls=%async_computation.26 | async-start | bytes 1310720 | tf_op jit(solution)/shard_map/reduce_scatter | solution.py:80
  444.0 131.9 %reduce-scatter.29.cloned.1.call-start = ((), (), s32[]{:S(2)}) async-start(), calls=%async_computation.28 | async-start | bytes 5242880 | tf_op jit(solution)/shard_map/reduce_scatter | solution.py:86
  450.3 173.1 %reduce-scatter.27.cloned.1.call-start = ((), (), s32[]{:S(2)}) async-start(), calls=%async_computation.27 | async-start | bytes 5242880 | tf_op jit(solution)/shard_map/reduce_scatter | solution.py:83
  456.6 207.5 %reduce-scatter.23.cloned.1.call-start = ((), (), s32[]{:S(2)}) async-start(), calls=%async_computation.25 | async-start | bytes 3932160 | tf_op jit(solution)/shard_map/reduce_scatter | solution.py:77
  506.3 211.1 %reduce-scatter.21.cloned.1.call-start = ((), (), s32[]{:S(2)}) async-start(), calls=%async_computation.23 | async-start | bytes 1572864 | tf_op jit(solution)/shard_map/reduce_scatter | solution.py:271
  512.3 299.7 %all-reduce.4.cloned.1.call-start = ((), (), s32[]{:S(2)}) async-start(), calls=%async_computation.29 | async-start | bytes 6291456 | tf_op jit(solution)/shard_map/psum | solution.py:68
  668.2 49.2 %copy-start.12 = (f32[256,1024]{1,0:T(8,128)S(1)}, f32[256,1024]{1,0:T(8,128)}, u32[]{:S(2)}) copy-start(f32[256,1024]{1,0:T(8,128)} %copy-done.11) | copy-start | bytes 3145732
  714.8 100.8 %copy-start.42 = (f32[8,1024]{1,0:T(8,128)}, f32[8,1024]{1,0:T(8,128)S(1)}, u32[]{:S(2)}) copy-start(f32[8,1024]{1,0:T(8,128)S(1)} %get-tuple-element.48) | copy-start | bytes 98308
  714.8 100.8 %copy-start.47 = (f32[4096]{0:T(1024)}, f32[4096]{0:T(1024)S(1)}, u32[]{:S(2)}) copy-start(f32[4096]{0:T(1024)S(1)} %get-tuple-element.49) | copy-start | bytes 49156
  (55 other events, 545.1 us)
Sparse Core Ops, SparseCore 0:
  10.2 31.6 all-gather.10
  48.3 45.6 all-gather.26
  96.2 44.4 all-gather.12
  142.7 15.6 all-gather.14
  161.4 20.3 reduce-scatter.10
  183.8 34.4 all-gather.18
  220.4 21.2 all-gather.16
  243.8 34.9 all-gather.20
  285.1 20.3 reduce-scatter.12
  310.1 21.2 all-gather.22
  343.3 20.3 reduce-scatter.14
  369.7 21.2 all-gather.24
  412.3 43.6 reduce-scatter.18
  458.7 42.8 reduce-scatter.16
  504.5 23.9 reduce-scatter.24
  531.4 44.3 reduce-scatter.28
  578.8 44.5 reduce-scatter.26
  626.4 37.7 reduce-scatter.22
  667.0 20.9 reduce-scatter.20
  690.4 121.4 all-reduce.3
where the time goes:
time: 859 us; the launch traced here: 855 us
  waiting for transfers between devices  546 us (64%)
  matrix products  140 us (16%)
  other arithmetic  70.4 us (8%)
  blocking collectives  41.5 us (5%)
  local copies, waits for them, and re-layouts  39.8 us (5%)
  between operations  15.3 us (2%)
    psum x1, waiting for transfers between devices, over_context(): lax.psum(grads[0].astype(jnp.bfloat16), 'context').astype(jnp.float32)  92.5 us
    reduce_scatter x1, waiting for transfers between devices, to_owner(): lax.psum_scatter(grads[2].astype(jnp.bfloat16), 'shard', scatter_dimensio...  47.6 us
    reduce_scatter x1, waiting for transfers between devices, to_owner(): lax.psum_scatter(grads[3].astype(jnp.bfloat16), 'shard', scatter_dimensio...  47.4 us
    psum x1, blocking collectives, on_device(): lax.psum((local_vectors, local_bias), ('shard', 'context', 'tensor'))  41.5 us
    reduce_scatter x1, waiting for transfers between devices, to_owner(): lax.psum_scatter(grads[0].astype(jnp.bfloat16), 'shard', scatter_dimensio...  40.7 us
    all_gather x1, waiting for transfers between devices, on_device(): lax.all_gather(key_half, 'context', axis=0, tiled=True)  39.4 us
    all_gather x1, waiting for transfers between devices, on_device(): lax.all_gather(attn_in.astype(jnp.bfloat16), 'shard', axis=1, tiled=True)  31.7 us
    reduce_scatter x1, waiting for transfers between devices, on_device(): lax.psum_scatter(jnp.stack(key_list, 1).astype(jnp.bfloat16), 'context',...  30.2 us
  transfers between devices with their start and end apart: 20, of which 18 were waited for; matrix products, arithmetic and copies ran while one was open for 17% of the time, Pallas kernels for 0%

commit v1 on v0

--- a/solution.py
+++ b/solution.py
@@ -64,8 +64,14 @@
 
 
 def over_context(grads):
+
+    def _play_shifts_all(block_here):
+        r1 = jax.lax.all_gather(block_here, axis_name="context")
+        last = jnp.sum(r1, 0)
+        return last
+
     return (
-        lax.psum(grads[0].astype(jnp.bfloat16), "context").astype(jnp.float32),
+        _play_shifts_all(grads[0].astype(jnp.bfloat16)).astype(jnp.float32),
         lax.psum(grads[1].astype(jnp.bfloat16), "context").astype(jnp.float32),
         lax.psum(grads[2].astype(jnp.bfloat16), "context").astype(jnp.float32),
         lax.psum(grads[3].astype(jnp.bfloat16), "context").astype(jnp.float32),

time: 859 us -> 1030 us (1.20)
  waiting for transfers between devices: 546 us -> 703 us
    all_gather x0 -> x1, waiting for transfers between devices: none -> 214 us  [_play_shifts_all(): r1 = jax.lax.all_gather(block_here, axis_name='context')]
    psum x1, waiting for transfers between devices: 92.5 us -> 61.3 us  [over_context(): lax.psum(grads[1].astype(jnp.bfloat16), 'context').astype(jnp.float32)]
    reduce_scatter x1, waiting for transfers between devices: 40.7 us -> 19.3 us  [to_owner(): lax.psum_scatter(grads[0].astype(jnp.bfloat16), 'shard', scatter_dimensio...]
    unnamed x124 -> x121, local copies, waits for them, and re-layouts: 24.8 us -> 30.5 us
  transfers between devices with their start and end apart: 20 -> 21, of which waited for: 18 -> 19; matrix products, arithmetic and copies ran while one was open for 17% -> 17% of each run, Pallas kernels for 0% -> 0%
where the time goes in v1:
time: 1030 us; the launch traced here: 1020 us
  waiting for transfers between devices  703 us (68%)
  matrix products  140 us (14%)
  other arithmetic  69.5 us (7%)
  local copies, waits for them, and re-layouts  48.9 us (5%)
  blocking collectives  42.3 us (4%)
  between operations  15.1 us (1%)
    all_gather x1, waiting for transfers between devices, _play_shifts_all(): r1 = jax.lax.all_gather(block_here, axis_name='context')  214 us
    psum x1, waiting for transfers between devices, over_context(): lax.psum(grads[1].astype(jnp.bfloat16), 'context').astype(jnp.float32)  61.3 us
    reduce_scatter x1, waiting for transfers between devices, to_owner(): lax.psum_scatter(grads[2].astype(jnp.bfloat16), 'shard', scatter_dimensio...  47.6 us
    reduce_scatter x1, waiting for transfers between devices, to_owner(): lax.psum_scatter(grads[3].astype(jnp.bfloat16), 'shard', scatter_dimensio...  47.4 us
    psum x1, blocking collectives, on_device(): lax.psum((local_vectors, local_bias), ('shard', 'context', 'tensor'))  42.3 us
    all_gather x1, waiting for transfers between devices, on_device(): lax.all_gather(key_half, 'context', axis=0, tiled=True)  39.3 us
    all_gather x1, waiting for transfers between devices, on_device(): lax.all_gather(attn_in.astype(jnp.bfloat16), 'shard', axis=1, tiled=True)  31.7 us
    unnamed x121, local copies, waits for them, and re-layouts  30.5 us
  transfers between devices with their start and end apart: 21, of which 19 were waited for; matrix products, arithmetic and copies ran while one was open for 17% of the time, Pallas kernels for 0%

profile of v1, /device:TPU:0, one launch (start us, length us, event | category | flops | bytes accessed | tf_op | source)
XLA Modules:
  0.0 1021.2 jit_solution(17655979971790409259)
XLA Ops:
  10.2 31.7 %all-gather.13.cloned.1.call-done = bf16[3,1024,512]{1,2,0:T(8,128)(2,1)} async-done(((bf16[3,256,512]{1,2,0:T(8,128)(2,1)}), bf16[3,1024,512]{1,2,0:T(8,128)(2,1)}) %all-gather.13.cloned.1.call-update) | async-done | bytes 3145744 | tf_op jit(solution)/shard_map/all_gather | solution.py:131
  54.7 39.3 %all-gather.29.cloned.1.call-done = bf16[1,2048,512]{1,2,0:T(8,128)(2,1)} async-done(((bf16[1,512,512]{1,2,0:T(8,128)(2,1)}), bf16[1,2048,512]{1,2,0:T(8,128)(2,1)}) %all-gather.29.cloned.1.call-update) | async-done | bytes 2097168 | tf_op jit(solution)/shard_map/all_gather | solution.py:148
  94.0 16.0 %fusion.1 = (f32[8,512]{1,0:T(8,128)S(1)}, f32[8,512,2048]{2,1,0:T(8,128)}) fusion(pred[512,2048]{1,0:T(8,128)(4,1)S(1)} %broadcast_compare_fusion, bf16[2048,8,64]{0,2,1:T(8,128)(2,1)} %bitcast.209, f32[512,8,64]{0,2,1:T(8,128)} %bitcast.9, f32[8,64]{1,0:T(8,128)S(1)} %add.259), kind=kOutput, calls=%fused_computation.5 | convolution fusion | flops 1099427840 | bytes 37767168 | tf_op jit(solution)/shard_map/qhd,khd->hqk/dot_general | solution.py:160
  110.0 15.1 %exponential_reduce_fusion = f32[8,512]{1,0:T(8,128)S(1)} fusion(f32[8,512,2048]{2,1,0:T(8,128)} %get-tuple-element.96, f32[8,512]{1,0:T(8,128)S(1)} %get-tuple-element.95, pred[512,2048]{1,0:T(8,128)(4,1)S(1)} %broadcast_compare_fusion), kind=kLoop, calls=%fused_computation.2 | loop fusion | flops 33550336 | bytes 34635776 | tf_op jit(solution)/shard_map/reduce_sum | solution.py:177
  125.2 15.5 %all-gather.15.cloned.1.call-done = bf16[2048,1,512]{0,2,1:T(8,128)(2,1)} async-done(((bf16[512,1,512]{0,2,1:T(8,128)(2,1)}), bf16[2048,1,512]{0,2,1:T(8,128)(2,1)}) %all-gather.15.cloned.1.call-update) | async-done | bytes 2097168 | tf_op jit(solution)/shard_map/all_gather | solution.py:149
  140.7 16.4 %fusion.57 = (bf16[512,8,64]{0,2,1:T(8,128)(2,1)S(1)}, f32[512,8,64]{0,2,1:T(8,128)}) fusion(bf16[2048,8,64]{0,2,1:T(8,128)(2,1)} %bitcast.250, f32[8,512,2048]{2,1,0:T(8,128)} %get-tuple-element.96, f32[8,512]{1,0:T(8,128)S(1)} %log_add_fusion, pred[512,2048]{1,0:T(8,128)(4,1)S(1)} %broadcast_compare_fusion), kind=kOutput, calls=%fused_computation.137 | convolution fusion | flops 1107558400 | bytes 38289408 | tf_op jit(solution)/shard_map/hqk,khd->qhd/dot_general | solution.py:180
  164.2 17.6 %reduce-scatter.11.cloned.1.call-done = bf16[256,1024]{1,0:T(8,128)(2,1)} async-done(((bf16[512,1024]{1,0:T(8,128)(2,1)}), bf16[256,1024]{1,0:T(8,128)(2,1)}) %reduce-scatter.11.cloned.1.call-update) | async-done | bytes 524304 | tf_op jit(solution)/shard_map/reduce_scatter | solution.py:189
  189.0 29.2 %all-gather.21.cloned.1.call-done = bf16[1024,2048]{1,0:T(8,128)(2,1)} async-done(((bf16[256,2048]{1,0:T(8,128)(2,1)}), bf16[1024,2048]{1,0:T(8,128)(2,1)}) %all-gather.21.cloned.1.call-update) | async-done | bytes 4194320 | tf_op jit(solution)/shard_map/all_gather | solution.py:133
  218.3 23.4 %all-gather.19.cloned.1.call-done = bf16[512,1024]{1,0:T(8,128)(2,1)} async-done(((bf16[256,1024]{1,0:T(8,128)(2,1)}), bf16[512,1024]{1,0:T(8,128)(2,1)}) %all-gather.19.cloned.1.call-update) | async-done | bytes 1048592 | tf_op jit(solution)/shard_map/all_gather | solution.py:198
  249.6 29.3 %all-gather.23.cloned.1.call-done = bf16[2048,1024]{1,0:T(8,128)(2,1)} async-done(((bf16[2048,256]{1,0:T(8,128)(2,1)}), bf16[2048,1024]{1,0:T(8,128)(2,1)}) %all-gather.23.cloned.1.call-update) | async-done | bytes 4194320 | tf_op jit(solution)/shard_map/all_gather | solution.py:134
  285.1 20.5 %reduce-scatter.13.cloned.1.call-done = bf16[256,1024]{1,0:T(8,128)(2,1)} async-done(((bf16[512,1024]{1,0:T(8,128)(2,1)}), bf16[256,1024]{1,0:T(8,128)(2,1)}) %reduce-scatter.13.cloned.1.call-update) | async-done | bytes 524304 | tf_op jit(solution)/shard_map/reduce_scatter | solution.py:201
  310.0 21.4 %all-gather.25.cloned.1.call-done = bf16[512,1024]{1,0:T(8,128)(2,1)} async-done(((bf16[256,1024]{1,0:T(8,128)(2,1)}), bf16[512,1024]{1,0:T(8,128)(2,1)}) %all-gather.25.cloned.1.call-update) | async-done | bytes 1048592 | tf_op jit(solution)/shard_map/all_gather | solution.py:213
  343.2 20.5 %reduce-scatter.15.cloned.1.call-done = bf16[256,1024]{1,0:T(8,128)(2,1)} async-done(((bf16[512,1024]{1,0:T(8,128)(2,1)}), bf16[256,1024]{1,0:T(8,128)(2,1)}) %reduce-scatter.15.cloned.1.call-update) | async-done | bytes 524304 | tf_op jit(solution)/shard_map/reduce_scatter | solution.py:218
  369.7 21.2 %all-gather.27.cloned.1.call-done = bf16[512,1024]{1,0:T(8,128)(2,1)} async-done(((bf16[256,1024]{1,0:T(8,128)(2,1)}), bf16[512,1024]{1,0:T(8,128)(2,1)}) %all-gather.27.cloned.1.call-update) | async-done | bytes 1048592 | tf_op jit(solution)/shard_map/all_gather | solution.py:225
  394.3 15.3 %convolution_convert_fusion.2 = bf16[8,64,2048]{2,1,0:T(8,128)(2,1)S(1)} fusion(bf16[512,8,64]{0,2,1:T(8,128)(2,1)} %bitcast.215, f32[8,512,2048]{2,1,0:T(8,128)} %get-tuple-element.96, f32[8,512]{1,0:T(8,128)S(1)} %log_add_fusion, pred[512,2048]{1,0:T(8,128)(4,1)S(1)} %broadcast_compare_fusion), kind=kOutput, calls=%fused_computation.22 | convolution fusion | flops 1108344832 | bytes 37240832 | tf_op jit(solution)/shard_map/hqk,qhd->khd/dot_general | solution.py:257
  412.2 17.9 %multiply_convert_fusion = bf16[8,512,2048]{2,1,0:T(8,128)(2,1)S(1)} fusion(f32[8,512,2048]{2,1,0:T(8,128)} %get-tuple-element.96, bf16[512,8,64]{0,2,1:T(8,128)(2,1)} %bitcast.216, bf16[2048,8,64]{0,2,1:T(8,128)(2,1)} %bitcast.251, f32[8,512]{1,0:T(8,128)} %bitcast.237, f32[8,512]{1,0:T(8,128)} %copy-done.44, pred[512,2048]{1,0:T(8,128)(4,1)S(1)} %broadcast_compare_fusion), kind=kOutput, calls=%fused_computation | convolution fusion | flops 1132462080 | bytes 54034432 | tf_op jit(solution)/shard_map/qhd,khd->hqk/dot_general | solution.py:244
  458.2 11.8 %fusion.55 = (f32[8,64]{1,0:T(8,128)S(1)}, bf16[512,8,64]{0,2,1:T(8,128)(2,1)}) fusion(bf16[2048,8,64]{0,2,1:T(8,128)(2,1)S(1)} %bitcast.210, bf16[8,512,2048]{2,1,0:T(8,128)(2,1)} %copy-done), kind=kOutput, calls=%fused_computation.135 | convolution fusion | flops 1074265600 | bytes 19400704 | tf_op jit(solution)/shard_map/hqk,khd->qhd/dot_general | solution.py:247
  471.3 30.2 %reduce-scatter.17.cloned.1.call-done = bf16[512,1,512]{2,0,1:T(8,128)(2,1)} async-done(((bf16[2048,1,512]{2,0,1:T(8,128)(2,1)}), bf16[512,1,512]{2,0,1:T(8,128)(2,1)}) %reduce-scatter.17.cloned.1.call-update) | async-done | bytes 524304 | tf_op jit(solution)/shard_map/reduce_scatter | solution.py:263
  528.5 47.4 %reduce-scatter.29.cloned.1.call-done = bf16[2048,256]{1,0:T(8,128)(2,1)} async-done(((bf16[2048,1024]{1,0:T(8,128)(2,1)}), bf16[2048,256]{1,0:T(8,128)(2,1)}) %reduce-scatter.29.cloned.1.call-update) | async-done | bytes 1048592 | tf_op jit(solution)/shard_map/reduce_scatter | solution.py:92
  575.9 47.6 %reduce-scatter.27.cloned.1.call-done = bf16[256,2048]{1,0:T(8,128)(2,1)} async-done(((bf16[1024,2048]{1,0:T(8,128)(2,1)}), bf16[256,2048]{1,0:T(8,128)(2,1)}) %reduce-scatter.27.cloned.1.call-update) | async-done | bytes 1048592 | tf_op jit(solution)/shard_map/reduce_scatter | solution.py:89
  629.0 214.1 %all-gather.31.cloned.1.call-done = bf16[12,1024,512]{2,1,0:T(8,128)(2,1)} async-done(((bf16[3,1024,512]{2,1,0:T(8,128)(2,1)}), bf16[12,1024,512]{2,1,0:T(8,128)(2,1)}) %all-gather.31.cloned.1.call-update) | async-done | bytes 12582928 | tf_op jit(solution)/shard_map/all_gather | solution.py:69
  854.9 42.3 %all-reduce = (f32[8,1024]{1,0:T(8,128)S(1)}, f32[4096]{0:T(1024)S(1)}) all-reduce(f32[8,1024]{1,0:T(8,128)S(1)} %stack.97, f32[4096]{0:T(1024)S(1)} %dynamic_update_slice.13), channel_id=1, replica_groups=mesh['shard'=4,'context'=4,'tensor'=2] {'shard','context','tensor'}, use_global_device_ids=true, to_apply=%region_33.34 | all-reduce | flops 12288 | bytes 98304 | tf_op jit(solution)/shard_map/psum | solution.py:310
  901.8 61.3 %all-reduce.4.cloned.1.call-done = (bf16[512,256]{1,0:T(8,128)(2,1)}, bf16[256,2048]{1,0:T(8,128)(2,1)}, bf16[2048,256]{1,0:T(8,128)(2,1)}) async-done(((bf16[512,256]{1,0:T(8,128)(2,1)}, bf16[256,2048]{1,0:T(8,128)(2,1)}, bf16[2048,256]{1,0:T(8,128)(2,1)}), (bf16[512,256]{1,0:T(8,128)(2,1)}, bf16[256,2048]{1,0:T(8,128)(2,1)}, bf16[2048,256]{1,0:T(8,128)(2,1)})) %all-reduce.4.cloned.1.call-update) | async-done | bytes 2359312 | tf_op jit(solution)/shard_map/psum | solution.py:75
  983.7 19.3 %reduce-scatter.23.cloned.1.call-done = bf16[3,256,512]{1,2,0:T(8,128)(2,1)} async-done(((bf16[3,1024,512]{1,2,0:T(8,128)(2,1)}), bf16[3,256,512]{1,2,0:T(8,128)(2,1)}) %reduce-scatter.23.cloned.1.call-update) | async-done | bytes 786448 | tf_op jit(solution)/shard_map/reduce_scatter | solution.py:83
  (245 shorter events, 181.6 us)
Async XLA Ops:
  7.2 34.7 %all-gather.13.cloned.1.call-start = ((), (), s32[]{:S(2)}) async-start(), calls=%async_computation.10 | async-start | bytes 3932160 | tf_op jit(solution)/shard_map/all_gather | solution.py:131
  10.1 83.9 %all-gather.29.cloned.1.call-start = ((), (), s32[]{:S(2)}) async-start(), calls=%async_computation.25 | async-start | bytes 2621440 | tf_op jit(solution)/shard_map/all_gather | solution.py:148
  48.2 92.5 %all-gather.15.cloned.1.call-start = ((), (), s32[]{:S(2)}) async-start(), calls=%async_computation.11 | async-start | bytes 2621440 | tf_op jit(solution)/shard_map/all_gather | solution.py:149
  50.5 107.8 %all-gather.17.cloned.1.call-start = ((), (), s32[]{:S(2)}) async-start(), calls=%async_computation.12 | async-start | bytes 1310720 | tf_op jit(solution)/shard_map/all_gather | solution.py:132
  51.3 130.5 %reduce-scatter.11.cloned.1.call-start = ((), (), s32[]{:S(2)}) async-start(), calls=%async_computation.13 | async-start | bytes 1572864 | tf_op jit(solution)/shard_map/reduce_scatter | solution.py:189
  125.2 269.2 %copy-start.44 = (f32[8,512]{1,0:T(8,128)}, f32[8,512]{1,0:T(8,128)S(1)}, u32[]{:S(2)}) copy-start(f32[8,512]{1,0:T(8,128)S(1)} %log_add_fusion) | copy-start | bytes 49156
  161.3 57.0 %all-gather.21.cloned.1.call-start = ((), (), s32[]{:S(2)}) async-start(), calls=%async_computation.15 | async-start | bytes 5242880 | tf_op jit(solution)/shard_map/all_gather | solution.py:133
  164.1 77.6 %all-gather.19.cloned.1.call-start = ((), (), s32[]{:S(2)}) async-start(), calls=%async_computation.14 | async-start | bytes 1572864 | tf_op jit(solution)/shard_map/all_gather | solution.py:198
  185.7 93.2 %all-gather.23.cloned.1.call-start = ((), (), s32[]{:S(2)}) async-start(), calls=%async_computation.16 | async-start | bytes 5242880 | tf_op jit(solution)/shard_map/all_gather | solution.py:134
  188.4 117.1 %reduce-scatter.13.cloned.1.call-start = ((), (), s32[]{:S(2)}) async-start(), calls=%async_computation.17 | async-start | bytes 1572864 | tf_op jit(solution)/shard_map/reduce_scatter | solution.py:201
  285.0 46.3 %all-gather.25.cloned.1.call-start = ((), (), s32[]{:S(2)}) async-start(), calls=%async_computation.18 | async-start | bytes 1572864 | tf_op jit(solution)/shard_map/all_gather | solution.py:213
  310.0 53.7 %reduce-scatter.15.cloned.1.call-start = ((), (), s32[]{:S(2)}) async-start(), calls=%async_computation.19 | async-start | bytes 1572864 | tf_op jit(solution)/shard_map/reduce_scatter | solution.py:218
  343.1 47.8 %all-gather.27.cloned.1.call-start = ((), (), s32[]{:S(2)}) async-start(), calls=%async_computation.20 | async-start | bytes 1572864 | tf_op jit(solution)/shard_map/all_gather | solution.py:225
  369.5 101.7 %reduce-scatter.19.cloned.1.call-start = ((), (), s32[]{:S(2)}) async-start(), calls=%async_computation.22 | async-start | bytes 2621440 | tf_op jit(solution)/shard_map/reduce_scatter | solution.py:266
  412.2 89.4 %reduce-scatter.17.cloned.1.call-start = ((), (), s32[]{:S(2)}) async-start(), calls=%async_computation.21 | async-start | bytes 2621440 | tf_op jit(solution)/shard_map/reduce_scatter | solution.py:263
  441.0 87.5 %reduce-scatter.25.cloned.1.call-start = ((), (), s32[]{:S(2)}) async-start(), calls=%async_computation.27 | async-start | bytes 1310720 | tf_op jit(solution)/shard_map/reduce_scatter | solution.py:86
  444.0 131.9 %reduce-scatter.29.cloned.1.call-start = ((), (), s32[]{:S(2)}) async-start(), calls=%async_computation.29 | async-start | bytes 5242880 | tf_op jit(solution)/shard_map/reduce_scatter | solution.py:92
  450.3 173.1 %reduce-scatter.27.cloned.1.call-start = ((), (), s32[]{:S(2)}) async-start(), calls=%async_computation.28 | async-start | bytes 5242880 | tf_op jit(solution)/shard_map/reduce_scatter | solution.py:89
  456.6 386.4 %all-gather.31.cloned.1.call-start = ((), (), s32[]{:S(2)}) async-start(), calls=%async_computation.26 | async-start | bytes 15728640 | tf_op jit(solution)/shard_map/all_gather | solution.py:69
  511.0 388.9 %reduce-scatter.21.cloned.1.call-start = ((), (), s32[]{:S(2)}) async-start(), calls=%async_computation.23 | async-start | bytes 1572864 | tf_op jit(solution)/shard_map/reduce_scatter | solution.py:277
  516.9 446.3 %all-reduce.4.cloned.1.call-start = ((), (), s32[]{:S(2)}) async-start(), calls=%async_computation.30 | async-start | bytes 4718592 | tf_op jit(solution)/shard_map/psum | solution.py:75
  623.4 379.6 %reduce-scatter.23.cloned.1.call-start = ((), (), s32[]{:S(2)}) async-start(), calls=%async_computation.24 | async-start | bytes 3932160 | tf_op jit(solution)/shard_map/reduce_scatter | solution.py:83
  854.2 109.0 %copy-start.22 = (f32[2,512,256]{2,1,0:T(8,128)S(1)}, f32[2,512,256]{2,1,0:T(8,128)}, u32[]{:S(2)}) copy-start(f32[2,512,256]{2,1,0:T(8,128)} %param.25) | copy-start | bytes 3145732
  897.2 67.0 %copy-start.40 = (f32[8,1024]{1,0:T(8,128)}, f32[8,1024]{1,0:T(8,128)S(1)}, u32[]{:S(2)}) copy-start(f32[8,1024]{1,0:T(8,128)S(1)} %get-tuple-element.48) | copy-start | bytes 98308
  (54 other events, 719.6 us)
Sparse Core Ops, SparseCore 0:
  10.2 31.6 all-gather.12
  48.3 45.6 all-gather.28
  96.2 44.4 all-gather.14
  142.7 15.6 all-gather.16
  161.4 20.3 reduce-scatter.10
  183.8 34.4 all-gather.20
  220.4 21.2 all-gather.18
  243.8 34.9 all-gather.22
  285.1 20.3 reduce-scatter.12
  310.1 21.2 all-gather.24
  343.3 20.3 reduce-scatter.14
  369.6 21.2 all-gather.26
  412.3 43.6 reduce-scatter.18
  458.7 42.8 reduce-scatter.16
  504.5 23.9 reduce-scatter.24
  531.4 44.3 reduce-scatter.28
  578.8 44.5 reduce-scatter.26
  624.8 218.1 all-gather.30
  845.9 19.0 reduce-scatter.20
  867.4 95.6 all-reduce.3
  966.3 36.7 reduce-scatter.22
